TPU v7x, 128 devices: a whole 4x4x4 slice. The times are simulated.
128 devices in a mesh: grp: 8 (over y, core), dom: 16 (over z, x).
Axes of the slice: x: 4, y: 4, z: 4, core: 2. Of those that a mesh axis runs over, the one named last changes fastest.
Arguments:
- diag_blocks: bfloat16 [2048, 384, 384], P(('grp', 'dom')), may hold values from -0.3125 to 0.3125
- face_in: bfloat16 [4096, 384, 384], P(('grp', 'dom')), may hold values from -0.3125 to 0.3125
- face_cross: bfloat16 [2048, 384, 384], P(('grp', 'dom')), may hold values from -0.3125 to 0.3125
- metric: float32 [2048, 384], P(('grp', 'dom')), may hold values from 0.5 to 2
- source_in: int32 [4096], P(('grp', 'dom')), may hold values from 0 to 15
- source_cross: int32 [2048], P(('grp', 'dom')), may hold values from 0 to 15
- orient_in: int32 [4096], P(('grp', 'dom')), may hold values from 0 to 7
- orient_cross: int32 [2048], P(('grp', 'dom')), may hold values from 0 to 7
- peer_in: int32 [4096, 1], P(('grp', 'dom')), may hold values from 0 to 15; in each aligned block of 32 rows (0 to 31, 32 to 63, ...) at most 3 rows name the same one
- peer_cross: int32 [2048, 1], P(('grp', 'dom')), may hold values from 0 to 7; in each aligned block of 16 rows (0 to 15, 16 to 31, ...) at most 3 rows name the same one
- target_in: int32 [4096], P(('grp', 'dom')), may hold values from 0 to 47
- target_cross: int32 [2048], P(('grp', 'dom')), may hold values from 0 to 47
Outputs:
- coarse_diag: float32 [2048, 2304], P('grp')
- coarse_face: float32 [2048, 6912], P('grp')
Inputs may be any that keep to these rules, and one draw needn't show every extreme that they name: `peer_in`: at most 3 records of one device name the same partition; on some device exactly 3 do. `peer_cross`: at most 3 records of one device name the same group; on some device exactly 3 do.
All inputs are finite; a program needn't handle non-finite values.
Results may differ from a plain program's by a relative error of at most 0.0052.
Values may be sent and summed in bfloat16 or wider, within the bound.
A program may use at most 128 MiB of HBM per device.

v0:
```python
import jax
import jax.numpy as jnp
from jax import lax
from jax.sharding import PartitionSpec as P

CROSS_CAP = 3


def corner_table(var_count):
    nodes = -1.0 + 2.0 * jnp.arange(4, dtype=jnp.float32) / 3.0
    basis = jnp.stack(((1.0 - nodes) / 2.0, (1.0 + nodes) / 2.0), axis=1)
    cube = jnp.einsum("ia,jb,kc->abcijk", basis, basis, basis).reshape(8, 64)
    return jnp.kron(jnp.eye(var_count, dtype=jnp.float32), cube)


def restrictor(weights, orient):
    var_count = weights.shape[1] // 64
    table = corner_table(var_count)
    full = weights[:, None, :] * table[None]
    shaped = full.reshape(weights.shape[0], var_count * 8, var_count, 4, 4, 4)
    bits = orient.reshape(-1, 1, 1, 1, 1, 1)
    shaped = jnp.where(bits % 2 == 1, jnp.flip(shaped, 3), shaped)
    shaped = jnp.where(bits // 2 % 2 == 1, jnp.flip(shaped, 4), shaped)
    shaped = jnp.where(bits // 4 % 2 == 1, jnp.flip(shaped, 5), shaped)
    return shaped.reshape(weights.shape[0], var_count * 8, var_count * 64).astype(jnp.bfloat16)


def plain_restrictor(weights):
    table = corner_table(weights.shape[1] // 64)
    return (weights[:, None, :] * table[None]).astype(jnp.bfloat16)


def pick_rows(index, table):
    picks = (index[:, None] == jnp.arange(table.shape[0], dtype=jnp.int32)[None, :]).astype(
        jnp.float32
    )
    return jnp.dot(picks, table, precision=lax.Precision.HIGHEST)


def one_sided(blocks, column_side):
    return jnp.einsum(
        "rcj,rij->rci", column_side, blocks, preferred_element_type=jnp.float32
    ).astype(jnp.bfloat16)


def coarse_terms(row_side, products):
    return jnp.einsum("rci,rdi->rcd", row_side, products, preferred_element_type=jnp.float32)


def id_row(values, width):
    flat = values.reshape(-1).astype(jnp.bfloat16)
    return jnp.pad(flat, (0, width - flat.shape[0]))[None, :]


def per_device(
    diag_blocks,
    face_in,
    face_cross,
    metric,
    source_in,
    source_cross,
    orient_in,
    orient_cross,
    peer_in,
    peer_cross,
    target_in,
    target_cross,
):
    elem_count = metric.shape[0]
    coarse_width = metric.shape[1] // 8
    square = coarse_width * coarse_width
    slots_dev = 3 * elem_count
    group_width = lax.axis_size("dom")
    group_count = lax.axis_size("grp")
    my_dom = lax.axis_index("dom")
    my_grp = lax.axis_index("grp")
    inner_count = face_in.shape[0]
    cross_count = face_cross.shape[0]
    metric_dom = lax.all_gather(metric, "dom", axis=0, tiled=True)
    metric_grp = lax.all_gather(metric, "grp", axis=0, tiled=True)
    diag_side = plain_restrictor(metric)
    diag_c = coarse_terms(diag_side, one_sided(diag_blocks, diag_side))
    diag_rows = diag_c.reshape(elem_count, square).astype(jnp.bfloat16)
    diag_all = lax.all_gather(diag_rows, "dom", axis=0, tiled=True)
    cross_y = one_sided(face_cross, restrictor(pick_rows(source_cross, metric), orient_cross))
    peer_x = peer_cross[:, 0]
    cross_row_side = plain_restrictor(
        pick_rows(peer_x * elem_count + target_cross // 3, metric_grp)
    )
    cross_c = coarse_terms(cross_row_side, cross_y).reshape(cross_count, square)
    cross_ids = jnp.stack((peer_x, target_cross), axis=1)
    cross_packet = jnp.concatenate(
        (cross_c.astype(jnp.bfloat16), id_row(cross_ids, square)), axis=0
    )
    cross_got = lax.all_gather(cross_packet, "grp", axis=0)
    got_rows = cross_got[:, :cross_count, :]
    got_ids = cross_got[:, cross_count, : 2 * cross_count].astype(jnp.int32)
    got_peer = got_ids[:, 0::2]
    got_target = got_ids[:, 1::2]
    match = got_peer == my_grp
    rank = jnp.cumsum(match.astype(jnp.int32), axis=1) - 1
    picks = match[:, None, :] & (
        rank[:, None, :] == jnp.arange(CROSS_CAP, dtype=jnp.int32)[None, :, None]
    )
    mine_rows = (
        jnp.einsum(
            "skr,srq->skq", picks.astype(jnp.bfloat16), got_rows, preferred_element_type=jnp.float32
        )
        .astype(jnp.bfloat16)
        .reshape(group_count * CROSS_CAP, square)
    )
    mine_target = jnp.sum(jnp.where(picks, got_target[:, None, :], 0), axis=2)
    mine_slot = jnp.where(jnp.any(picks, axis=2), my_dom * slots_dev + mine_target, -1).reshape(-1)
    inner_y = one_sided(face_in, restrictor(pick_rows(source_in, metric), orient_in))
    peer_i = peer_in[:, 0]
    inner_row_side = plain_restrictor(pick_rows(peer_i * elem_count + target_in // 3, metric_dom))
    inner_c = coarse_terms(inner_row_side, inner_y).reshape(inner_count, square)
    inner_slot = peer_i * slots_dev + target_in
    slots = jnp.concatenate((inner_slot, mine_slot), axis=0)
    valid = slots >= 0
    slot_code = jnp.stack(
        (jnp.where(valid, slots // 32, -1), jnp.where(valid, slots % 32, 0)), axis=1
    )
    face_packet = jnp.concatenate(
        (inner_c.astype(jnp.bfloat16), mine_rows, id_row(slot_code, square)), axis=0
    )
    face_all = lax.all_gather(face_packet, "dom", axis=0)
    contrib_count = slots.shape[0]
    contrib = face_all[:, :contrib_count, :].reshape(group_width * contrib_count, square)
    codes = face_all[:, contrib_count, : 2 * contrib_count].astype(jnp.int32)
    hi = codes[:, 0::2].reshape(-1)
    lo = codes[:, 1::2].reshape(-1)
    got_slot = jnp.where(hi >= 0, hi * 32 + lo, -1)
    group_slots = group_width * slots_dev
    onehot = (jnp.arange(group_slots, dtype=jnp.int32)[:, None] == got_slot[None, :]).astype(
        jnp.bfloat16
    )
    face = jnp.dot(onehot, contrib, preferred_element_type=jnp.float32)
    coarse_diag = diag_all.astype(jnp.float32)
    coarse_face = face.reshape(group_width * elem_count, 3 * square)
    return (coarse_diag, coarse_face)


def solution(mesh):
    placed = (
        P(("grp", "dom"), None, None),
        P(("grp", "dom"), None, None),
        P(("grp", "dom"), None, None),
        P(("grp", "dom"), None),
        P(("grp", "dom")),
        P(("grp", "dom")),
        P(("grp", "dom")),
        P(("grp", "dom")),
        P(("grp", "dom"), None),
        P(("grp", "dom"), None),
        P(("grp", "dom")),
        P(("grp", "dom")),
    )
    return jax.shard_map(
        per_device,
        mesh=mesh,
        in_specs=placed,
        out_specs=(P("grp", None), P("grp", None)),
        check_vma=False,
    )
```

profile of v0, /device:TPU:1, one launch (start us, length us, event | category | flops | bytes accessed | tf_op | source)
XLA Modules:
  0.0 171.8 jit_solution(11630039760645675383)
XLA Ops:
  7.4 0.1 mul.188
  7.5 0.1 broadcast_multiply_fusion.3
  7.6 0.1 mul.191
  7.8 4.3 %fusion.26 = bf16[16,48,48]{2,1,0:T(8,128)(2,1)S(1)} fusion(bf16[16,384,384]{2,1,0:T(8,128)(2,1)} %param.12, f32[48,384]{1,0:T(8,128)S(1)} %mul.191, f32[16,384]{1,0:T(8,128)} %param.15), kind=kOutput, calls=%fused_computation.30 | convolution fusion | flops 256315392 | bytes 4890624 | tf_op jit(solution)/shard_map/rci,rdi->rcd/dot_general | solution.py:47
  12.0 0.9 convert_element_type.104
  13.1 0.1 copy.31
  13.2 14.6 %all_gather.23 = f32[128,384]{1,0:T(8,128)S(1)} all-gather(f32[16,384]{1,0:T(8,128)S(1)} %copy-done), channel_id=1, replica_groups=mesh['grp'=8,'dom'=16] {'grp'}, dimensions={0}, use_global_device_ids=true | all-gather | bytes 221184 | tf_op jit(solution)/shard_map/all_gather | solution.py:80
  27.8 0.1 mul.206
  28.1 0.4 fusion.43
  28.6 1.0 broadcast_multiply_fusion.1
  29.6 0.6 reverse_select_fusion.5
  30.2 0.7 reverse_select_fusion.4
  30.9 0.7 fusion.1
  31.6 0.2 fusion.42
  31.8 4.3 %fusion.27 = bf16[16,48,48]{2,1,0:T(8,128)(2,1)S(1)} fusion(bf16[16,384,384]{2,1,0:T(8,128)(2,1)} %param.14, bf16[16,48,384]{1,0,2:T(8,128)(2,1)S(1)} %bitcast.38, f32[16,384]{1,0:T(8,128)S(1)} %fusion.42, f32[48,384]{1,0:T(8,128)S(1)} %mul.191), kind=kOutput, calls=%fused_computation.31 | convolution fusion | flops 255725568 | bytes 5480448 | tf_op jit(solution)/shard_map/rci,rdi->rcd/dot_general | solution.py:47
  36.1 0.2 convert_element_type.117
  36.3 0.1 copy.36
  36.4 0.1 convert_element_type.118
  36.6 13.5 %all-gather.2 = bf16[8,17,2304]{2,1,0:T(8,128)(2,1)S(1)} all-gather(bf16[1,17,2304]{2,1,0:T(8,128)(2,1)S(1)} %maximum_bitcast_fusion.1), channel_id=2, replica_groups=mesh['grp'=8,'dom'=16] {'grp'}, dimensions={0}, use_global_device_ids=true | all-gather | bytes 705024 | tf_op jit(solution)/shard_map/all_gather | solution.py:95
  50.1 0.1 slice.25
  50.2 0.1 slice.27
  50.3 0.2 reduce_window_sum.11
  50.5 0.2 fusion.60
  50.7 0.2 convolution_convert_fusion
  50.9 20.3 %all_gather.22 = f32[256,384]{1,0:T(8,128)S(1)} all-gather(f32[16,384]{1,0:T(8,128)S(1)} %copy-done), channel_id=1, replica_groups=mesh['grp'=8,'dom'=16] {'dom'}, dimensions={0}, use_global_device_ids=true | all-gather | bytes 417792 | tf_op jit(solution)/shard_map/all_gather | solution.py:79
  71.2 0.2 select_reduce_fusion
  71.5 0.1 fusion.47
  71.6 0.1 copy.37
  71.7 0.1 convert_element_type.123
  71.9 0.1 reshape.525
  72.0 0.4 fusion.39
  72.4 1.9 %broadcast_multiply_fusion = bf16[32,48,6,4,4,4]{1,0,5,4,3,2:T(8,128)(2,1)S(1)} fusion(f32[48,6,4,4,4]{0,4,3,2,1:T(4,128)S(1)} %broadcast_multiply_fusion.2, f32[32,6,4,4,4]{0,4,3,2,1:T(4,128)S(1)} %bitcast.40), kind=kLoop, calls=%fused_computation.11 | loop fusion | flops 1179648 | bytes 1302528 | tf_op jit(solution)/shard_map/mul | solution.py:19
  74.4 0.3 fusion.37
  74.7 1.3 reverse_select_fusion.2
  76.0 1.5 reverse_select_fusion.1
  77.5 1.1 fusion
  78.6 8.9 %fusion.17 = bf16[32,48,48]{2,1,0:T(8,128)(2,1)} fusion(bf16[32,384,384]{2,1,0:T(8,128)(2,1)} %param.13, bf16[32,48,384]{1,0,2:T(8,128)(2,1)S(1)} %bitcast.37, f32[48,384]{1,0:T(8,128)S(1)} %mul.191, f32[32,384]{1,0:T(8,128)S(1)} %fusion.37), kind=kOutput, calls=%fused_computation.23 | convolution fusion | flops 511451136 | bytes 10887168 | tf_op jit(solution)/shard_map/rci,rdi->rcd/dot_general | solution.py:47
  87.5 1.4 convert_element_type.111
  88.9 0.7 maximum_bitcast_fusion
  89.7 2.8 %convert_element_type.105 = f32[256,2304]{1,0:T(8,128)} convert(bf16[256,2304]{1,0:T(8,128)(2,1)} %all-gather.7.cloned.1.call-done) | non-fusion elementwise | flops 589824 | bytes 3538944 | tf_op jit(solution)/shard_map/convert_element_type | solution.py:139
  92.5 54.4 %all-gather.9.cloned.1.call-done = bf16[16,57,2304]{2,1,0:T(8,128)(2,1)} async-done(((bf16[1,57,2304]{2,1,0:T(8,128)(2,1)}), bf16[16,57,2304]{2,1,0:T(8,128)(2,1)}) %all-gather.9.cloned.1.call-update) | async-done | bytes 4202512 | tf_op jit(solution)/shard_map/all_gather | solution.py:127
  146.9 0.8 slice_convert_fusion
  147.7 0.2 slice.29
  147.9 0.2 slice.30
  148.1 0.1 select_n.198
  148.2 2.2 %slice-done = bf16[16,56,2304]{2,1,0:T(8,128)(2,1)S(1)} async-done(((bf16[16,57,2304]{2,1,0:T(8,128)(2,1)}), bf16[16,56,2304]{2,1,0:T(8,128)(2,1)S(1)}, s32[]{:S(2)}) %slice-start) | async-done | bytes 4128792 | tf_op jit(solution)/shard_map/slice | solution.py:129
  150.4 6.0 %fusion.4 = f32[768,2304]{1,0:T(8,128)} fusion(bf16[896,2304]{1,0:T(8,128)(2,1)S(1)} %bitcast.39, s32[896]{0:T(1024)S(1)} %select_n.198), kind=kOutput, calls=%fused_computation.13 | convolution fusion | flops 3171581952 | bytes 11210240 | tf_op jit(solution)/shard_map/dot_general | solution.py:138
  156.3 8.6 %reshape.527 = f32[256,6912]{1,0:T(8,128)} reshape(f32[768,2304]{1,0:T(8,128)} %fusion.4) | data formatting | bytes 14155776 | tf_op jit(solution)/shard_map/reshape | solution.py:140
  (52 shorter events, 0.9 us)
Async XLA Ops:
  7.2 6.0 %copy-start = (f32[16,384]{1,0:T(8,128)S(1)}, f32[16,384]{1,0:T(8,128)}, u32[]{:S(2)}) copy-start(f32[16,384]{1,0:T(8,128)} %param.15) | copy-start | bytes 73732
  7.2 82.5 %all-gather.7.cloned.1.call-start = ((), (), s32[]{:S(2)}) async-start(), calls=%async_computation | async-start | bytes 1253376 | tf_op jit(solution)/shard_map/all_gather | solution.py:84
  7.7 20.4 %copy-start.1 = (s32[16]{0:T(128)S(1)}, s32[16]{0:T(128)}, u32[]{:S(2)}) copy-start(s32[16]{0:T(128)} %param.17) | copy-start | bytes 196
  7.7 20.7 %copy-start.3 = (s32[16]{0:T(128)S(1)}, s32[16]{0:T(128)}, u32[]{:S(2)}) copy-start(s32[16]{0:T(128)} %param.19) | copy-start | bytes 196
  7.7 20.7 %copy-start.5 = (s32[16,1]{0,1:T(1,128)S(1)}, s32[16,1]{0,1:T(1,128)}, u32[]{:S(2)}) copy-start(s32[16,1]{0,1:T(1,128)} %param.21) | copy-start | bytes 196
  7.8 20.8 %copy-start.4 = (s32[16]{0:T(128)S(1)}, s32[16]{0:T(128)}, u32[]{:S(2)}) copy-start(s32[16]{0:T(128)} %param.23) | copy-start | bytes 196
  12.9 134.0 %all-gather.9.cloned.1.call-start = ((), (), s32[]{:S(2)}) async-start(), calls=%async_computation.1 | async-start | bytes 5013504 | tf_op jit(solution)/shard_map/all_gather | solution.py:127
  31.8 39.7 %copy-start.6 = (s32[32]{0:T(128)S(1)}, s32[32]{0:T(128)}, u32[]{:S(2)}) copy-start(s32[32]{0:T(128)} %param.22) | copy-start | bytes 388
  31.8 39.7 %copy-start.7 = (s32[32,1]{0,1:T(1,128)S(1)}, s32[32,1]{0,1:T(1,128)}, u32[]{:S(2)}) copy-start(s32[32,1]{0,1:T(1,128)} %param.20) | copy-start | bytes 388
  31.8 40.2 %copy-start.2 = (s32[32]{0:T(128)S(1)}, s32[32]{0:T(128)}, u32[]{:S(2)}) copy-start(s32[32]{0:T(128)} %param.16) | copy-start | bytes 388
  36.6 37.8 %copy-start.8 = (s32[32]{0:T(128)S(1)}, s32[32]{0:T(128)}, u32[]{:S(2)}) copy-start(s32[32]{0:T(128)} %param.18) | copy-start | bytes 388
  148.2 2.2 %slice-start = ((bf16[16,57,2304]{2,1,0:T(8,128)(2,1)}), bf16[16,56,2304]{2,1,0:T(8,128)(2,1)S(1)}, s32[]{:S(2)}) async-start(bf16[16,57,2304]{2,1,0:T(8,128)(2,1)} %all-gather.9.cloned.1.call-done), calls=%async_computation.2 | async-start | bytes 8257536 | tf_op jit(solution)/shard_map/slice | solution.py:129
Sparse Core Ops, SparseCore 0:
  13.0 44.4 all-gather.6
  89.8 57.1 all-gather.8
where the time goes:
time: 172 us
  waiting for transfers between devices  54.5 us (32%)
  blocking collectives  48.4 us (28%)
  matrix products  24.8 us (14%)
  local copies, waits for them, and re-layouts  15.2 us (9%)
  between operations  14.4 us (8%)
  other arithmetic  14.3 us (8%)
    all_gather x1, waiting for transfers between devices, per_device(): face_all = lax.all_gather(face_packet, 'dom', axis=0)  54.4 us
    all_gather x1, blocking collectives, per_device(): metric_dom = lax.all_gather(metric, 'dom', axis=0, tiled=True)  20.3 us
    dot_general x3, matrix products, coarse_terms(): jnp.einsum('rci,rdi->rcd', row_side, products, preferred_element_type=jnp...  17.4 us
    all_gather x1, blocking collectives, per_device(): metric_grp = lax.all_gather(metric, 'grp', axis=0, tiled=True)  14.6 us
    all_gather x1, blocking collectives, per_device(): cross_got = lax.all_gather(cross_packet, 'grp', axis=0)  13.5 us
    reshape x1, local copies, waits for them, and re-layouts, per_device(): coarse_face = face.reshape(group_width * elem_count, 3 * square)  8.64 us
    dot_general x1, matrix products, per_device(): face = jnp.dot(onehot, contrib, preferred_element_type=jnp.float32)  5.97 us
  transfers between devices with their start and end apart: 2, of which 1 were waited for; matrix products, arithmetic and copies ran while one was open for 18% of the time, Pallas kernels for 0%

commit v1 on v0

--- a/solution.py
+++ b/solution.py
@@ -76,7 +76,11 @@
     my_grp = lax.axis_index("grp")
     inner_count = face_in.shape[0]
     cross_count = face_cross.shape[0]
-    metric_dom = lax.all_gather(metric, "dom", axis=0, tiled=True)
+    devices = lax.axis_size("dom")
+    repeats = [devices if d == 0 else 1 for d in range(metric.ndim)]
+    metric_dom = lax.all_to_all(
+        jnp.tile(metric, repeats), "dom", split_axis=0, concat_axis=0, tiled=True
+    )
     metric_grp = lax.all_gather(metric, "grp", axis=0, tiled=True)
     diag_side = plain_restrictor(metric)
     diag_c = coarse_terms(diag_side, one_sided(diag_blocks, diag_side))

time: 172 us -> 161 us (0.936)
  blocking collectives: 48.4 us -> 27.6 us
  starting transfers between devices: 0.08 us -> 8.54 us
  waiting for transfers between devices: 54.5 us -> 51.6 us
  local copies, waits for them, and re-layouts: 15.2 us -> 17.8 us
    all_gather x1 -> x0, blocking collectives: 20.3 us -> none  [per_device(): metric_dom = lax.all_gather(metric, 'dom', axis=0, tiled=True)]
    all_to_all x0 -> x1, starting transfers between devices: none -> 8.46 us  [per_device(): lax.all_to_all(jnp.tile(metric, repeats), 'dom', split_axis=0, concat_axi...]
    all_gather x1, waiting for transfers between devices: 54.4 us -> 51.6 us  [per_device(): face_all = lax.all_gather(face_packet, 'dom', axis=0)]
  transfers between devices with their start and end apart: 2 -> 3, of which waited for: 1 -> 1; matrix products, arithmetic and copies ran while one was open for 18% -> 23% of each run, Pallas kernels for 0% -> 0%
where the time goes in v1:
time: 161 us; the launch traced here: 160 us
  waiting for transfers between devices  51.6 us (32%)
  blocking collectives  27.6 us (17%)
  matrix products  25.8 us (16%)
  local copies, waits for them, and re-layouts  17.8 us (11%)
  between operations  14.5 us (9%)
  other arithmetic  14 us (9%)
  starting transfers between devices  8.54 us (5%)
    all_gather x1, waiting for transfers between devices, per_device(): face_all = lax.all_gather(face_packet, 'dom', axis=0)  51.6 us
    dot_general x3, matrix products, coarse_terms(): jnp.einsum('rci,rdi->rcd', row_side, products, preferred_element_type=jnp...  17.4 us
    all_gather x1, blocking collectives, per_device(): metric_grp = lax.all_gather(metric, 'grp', axis=0, tiled=True)  14.1 us
    all_gather x1, blocking collectives, per_device(): cross_got = lax.all_gather(cross_packet, 'grp', axis=0)  13.5 us
    reshape x1, local copies, waits for them, and re-layouts, per_device(): coarse_face = face.reshape(group_width * elem_count, 3 * square)  8.64 us
    all_to_all x1, starting transfers between devices, per_device(): lax.all_to_all(jnp.tile(metric, repeats), 'dom', split_axis=0, concat_axi...  8.46 us
    dot_general x1, matrix products, per_device(): face = jnp.dot(onehot, contrib, preferred_element_type=jnp.float32)  5.96 us
  transfers between devices with their start and end apart: 3, of which 1 were waited for; matrix products, arithmetic and copies ran while one was open for 23% of the time, Pallas kernels for 0%

profile of v1, /device:TPU:1, one launch (start us, length us, event | category | flops | bytes accessed | tf_op | source)
XLA Modules:
  0.0 159.8 jit_solution(4804956957874585707)
XLA Ops:
  7.2 1.5 tile.2
  8.7 8.5 %all-to-all-start = ((f32[16,16,384]{2,1,0:T(8,128)}), f32[16,16,384]{2,1,0:T(8,128)}, u32[]{:S(2)}, u32[]{:S(2)}) async-start(f32[16,16,384]{2,1,0:T(8,128)} %tile.2), calls=%async_computation | async-start | bytes 786432 | tf_op jit(solution)/shard_map/all_to_all | solution.py:81
  17.4 0.1 mul.188
  17.5 0.1 broadcast_multiply_fusion.3
  17.6 0.1 mul.191
  17.7 4.3 %fusion.26 = bf16[16,48,48]{2,1,0:T(8,128)(2,1)S(1)} fusion(bf16[16,384,384]{2,1,0:T(8,128)(2,1)} %param.12, f32[48,384]{1,0:T(8,128)S(1)} %mul.191, f32[16,384]{1,0:T(8,128)} %param.15), kind=kOutput, calls=%fused_computation.30 | convolution fusion | flops 256315392 | bytes 4890624 | tf_op jit(solution)/shard_map/rci,rdi->rcd/dot_general | solution.py:47
  22.0 0.8 convert_element_type.104
  23.0 0.1 copy.31
  23.1 14.1 %all_gather.19 = f32[128,384]{1,0:T(8,128)S(1)} all-gather(f32[16,384]{1,0:T(8,128)S(1)} %copy-done.2), channel_id=1, replica_groups=mesh['grp'=8,'dom'=16] {'grp'}, dimensions={0}, use_global_device_ids=true | all-gather | bytes 221184 | tf_op jit(solution)/shard_map/all_gather | solution.py:84
  37.2 0.1 mul.206
  37.5 0.4 fusion.43
  38.0 1.0 broadcast_multiply_fusion.1
  39.0 0.6 reverse_select_fusion.5
  39.6 0.7 reverse_select_fusion.4
  40.3 0.7 fusion.1
  41.0 0.2 fusion.42
  41.2 4.3 %fusion.27 = bf16[16,48,48]{2,1,0:T(8,128)(2,1)S(1)} fusion(bf16[16,384,384]{2,1,0:T(8,128)(2,1)} %param.14, bf16[16,48,384]{1,0,2:T(8,128)(2,1)S(1)} %bitcast.39, f32[16,384]{1,0:T(8,128)S(1)} %fusion.42, f32[48,384]{1,0:T(8,128)S(1)} %mul.191), kind=kOutput, calls=%fused_computation.31 | convolution fusion | flops 255725568 | bytes 5480448 | tf_op jit(solution)/shard_map/rci,rdi->rcd/dot_general | solution.py:47
  45.5 0.2 convert_element_type.117
  45.8 0.1 copy.36
  45.9 0.1 convert_element_type.118
  46.0 13.5 %all-gather.2 = bf16[8,17,2304]{2,1,0:T(8,128)(2,1)S(1)} all-gather(bf16[1,17,2304]{2,1,0:T(8,128)(2,1)S(1)} %maximum_bitcast_fusion.1), channel_id=2, replica_groups=mesh['grp'=8,'dom'=16] {'grp'}, dimensions={0}, use_global_device_ids=true | all-gather | bytes 705024 | tf_op jit(solution)/shard_map/all_gather | solution.py:99
  59.5 0.9 copy-done
  60.5 0.1 slice.27
  60.6 0.2 reduce_window_sum.11
  60.8 0.2 fusion.60
  61.0 0.2 select_reduce_fusion
  61.5 0.1 copy.37
  61.6 0.1 convert_element_type.123
  61.8 0.4 fusion.39
  62.1 2.1 %broadcast_multiply_fusion = bf16[32,48,6,4,4,4]{1,0,5,4,3,2:T(8,128)(2,1)S(1)} fusion(f32[48,6,4,4,4]{0,4,3,2,1:T(4,128)S(1)} %broadcast_multiply_fusion.2, f32[32,6,4,4,4]{0,4,3,2,1:T(4,128)S(1)} %bitcast.41), kind=kLoop, calls=%fused_computation.11 | loop fusion | flops 1179648 | bytes 1302528 | tf_op jit(solution)/shard_map/mul | solution.py:19
  64.3 1.0 reverse_select_fusion.2
  65.4 0.1 copy-done.1
  65.5 0.2 convolution_convert_fusion
  65.7 0.1 reshape.532
  65.8 1.3 reverse_select_fusion.1
  67.1 1.1 fusion
  68.2 1.3 fusion.37
  69.5 8.9 %fusion.17 = bf16[32,48,48]{2,1,0:T(8,128)(2,1)} fusion(bf16[32,384,384]{2,1,0:T(8,128)(2,1)} %param.13, bf16[32,48,384]{1,0,2:T(8,128)(2,1)S(1)} %bitcast.38, f32[48,384]{1,0:T(8,128)S(1)} %mul.191, f32[32,384]{1,0:T(8,128)S(1)} %fusion.37), kind=kOutput, calls=%fused_computation.23 | convolution fusion | flops 511451136 | bytes 10887168 | tf_op jit(solution)/shard_map/rci,rdi->rcd/dot_general | solution.py:47
  78.4 1.4 convert_element_type.111
  79.7 0.7 maximum_bitcast_fusion
  80.5 2.8 %convert_element_type.105 = f32[256,2304]{1,0:T(8,128)} convert(bf16[256,2304]{1,0:T(8,128)(2,1)} %all-gather.7.cloned.1.call-done) | non-fusion elementwise | flops 589824 | bytes 3538944 | tf_op jit(solution)/shard_map/convert_element_type | solution.py:143
  83.4 51.6 %all-gather.9.cloned.1.call-done = bf16[16,57,2304]{2,1,0:T(8,128)(2,1)} async-done(((bf16[1,57,2304]{2,1,0:T(8,128)(2,1)}), bf16[16,57,2304]{2,1,0:T(8,128)(2,1)}) %all-gather.9.cloned.1.call-update) | async-done | bytes 4202512 | tf_op jit(solution)/shard_map/all_gather | solution.py:131
  134.9 0.8 slice_convert_fusion
  135.7 0.2 slice.29
  135.9 0.2 slice.30
  136.2 2.2 %slice-done = bf16[16,56,2304]{2,1,0:T(8,128)(2,1)S(1)} async-done(((bf16[16,57,2304]{2,1,0:T(8,128)(2,1)}), bf16[16,56,2304]{2,1,0:T(8,128)(2,1)S(1)}, s32[]{:S(2)}) %slice-start) | async-done | bytes 4128792 | tf_op jit(solution)/shard_map/slice | solution.py:133
  138.3 6.0 %fusion.4 = f32[768,2304]{1,0:T(8,128)} fusion(bf16[896,2304]{1,0:T(8,128)(2,1)S(1)} %bitcast.40, s32[896]{0:T(1024)S(1)} %select_n.198), kind=kOutput, calls=%fused_computation.13 | convolution fusion | flops 3171581952 | bytes 11210240 | tf_op jit(solution)/shard_map/dot_general | solution.py:142
  144.3 8.6 %reshape.534 = f32[256,6912]{1,0:T(8,128)} reshape(f32[768,2304]{1,0:T(8,128)} %fusion.4) | data formatting | bytes 14155776 | tf_op jit(solution)/shard_map/reshape | solution.py:144
  (58 shorter events, 1.2 us)
Async XLA Ops:
  8.7 59.5 %all-to-all-start = ((f32[16,16,384]{2,1,0:T(8,128)}), f32[16,16,384]{2,1,0:T(8,128)}, u32[]{:S(2)}, u32[]{:S(2)}) async-start(f32[16,16,384]{2,1,0:T(8,128)} %tile.2), calls=%async_computation | async-start | bytes 786432 | tf_op jit(solution)/shard_map/all_to_all | solution.py:81
  17.1 6.0 %copy-start.2 = (f32[16,384]{1,0:T(8,128)S(1)}, f32[16,384]{1,0:T(8,128)}, u32[]{:S(2)}) copy-start(f32[16,384]{1,0:T(8,128)} %param.15) | copy-start | bytes 73732
  17.2 63.4 %all-gather.7.cloned.1.call-start = ((), (), s32[]{:S(2)}) async-start(), calls=%async_computation.1 | async-start | bytes 1253376 | tf_op jit(solution)/shard_map/all_gather | solution.py:88
  17.7 19.8 %copy-start.3 = (s32[16]{0:T(128)S(1)}, s32[16]{0:T(128)}, u32[]{:S(2)}) copy-start(s32[16]{0:T(128)} %param.17) | copy-start | bytes 196
  17.7 20.2 %copy-start.5 = (s32[16]{0:T(128)S(1)}, s32[16]{0:T(128)}, u32[]{:S(2)}) copy-start(s32[16]{0:T(128)} %param.19) | copy-start | bytes 196
  17.7 20.2 %copy-start.7 = (s32[16,1]{0,1:T(1,128)S(1)}, s32[16,1]{0,1:T(1,128)}, u32[]{:S(2)}) copy-start(s32[16,1]{0,1:T(1,128)} %param.21) | copy-start | bytes 196
  17.7 20.2 %copy-start.6 = (s32[16]{0:T(128)S(1)}, s32[16]{0:T(128)}, u32[]{:S(2)}) copy-start(s32[16]{0:T(128)} %param.23) | copy-start | bytes 196
  22.9 112.0 %all-gather.9.cloned.1.call-start = ((), (), s32[]{:S(2)}) async-start(), calls=%async_computation.2 | async-start | bytes 5013504 | tf_op jit(solution)/shard_map/all_gather | solution.py:131
  41.2 20.1 %copy-start.8 = (s32[32]{0:T(128)S(1)}, s32[32]{0:T(128)}, u32[]{:S(2)}) copy-start(s32[32]{0:T(128)} %param.22) | copy-start | bytes 388
  41.2 20.1 %copy-start.9 = (s32[32,1]{0,1:T(1,128)S(1)}, s32[32,1]{0,1:T(1,128)}, u32[]{:S(2)}) copy-start(s32[32,1]{0,1:T(1,128)} %param.20) | copy-start | bytes 388
  41.2 20.5 %copy-start.4 = (s32[32]{0:T(128)S(1)}, s32[32]{0:T(128)}, u32[]{:S(2)}) copy-start(s32[32]{0:T(128)} %param.16) | copy-start | bytes 388
  45.5 18.7 %copy-start.10 = (s32[32]{0:T(128)S(1)}, s32[32]{0:T(128)}, u32[]{:S(2)}) copy-start(s32[32]{0:T(128)} %param.18) | copy-start | bytes 388
  59.5 0.9 copy-start
  64.3 1.2 copy-start.1
  136.2 2.2 %slice-start = ((bf16[16,57,2304]{2,1,0:T(8,128)(2,1)}), bf16[16,56,2304]{2,1,0:T(8,128)(2,1)S(1)}, s32[]{:S(2)}) async-start(bf16[16,57,2304]{2,1,0:T(8,128)(2,1)} %all-gather.9.cloned.1.call-done), calls=%async_computation.3 | async-start | bytes 8257536 | tf_op jit(solution)/shard_map/slice | solution.py:133
Sparse Core Ops, SparseCore 0:
  23.0 43.2 all-gather.6
  80.6 54.2 all-gather.8
